TPU v7x, 256 devices: a whole 4x4x8 slice. The times are simulated.
256 devices in a mesh: vox: 64 (over y, x, z_lo), sen: 4 (over z_hi, core).
Axes of the slice: x: 4, y: 4, z: 8 (z_hi: 2, z_lo: 4; z = z_hi * 4 + z_lo), core: 2. Of those that a mesh axis runs over, the one named last changes fastest.
Arguments:
- image: float32 [64, 2, 512], P('vox'), may hold values from -6 to 6
- weights: bfloat16 [64, 4, 5, 1024, 1024], P('vox', 'sen'), may hold values from -0.0625 to 0.0625
- block_ids: int32 [64, 4, 5], P('vox', 'sen'), may hold values from 0 to 15
- offsets: int32 [64, 4, 5], P('vox', 'sen'), may hold values from 0 to 1984
- counts: int32 [64, 4], P('vox', 'sen'), may hold values from 1 to 5, as said below
- measured: bfloat16 [4, 256, 2048], P('sen', 'vox'), may hold values from -6 to 6
Outputs:
- image_next: float32 [64, 2, 512], P('vox')
- residual: float32 [4, 256, 2048], P('sen', 'vox')
Inputs may be any that keep to these rules, and one draw needn't show every extreme that they name: `counts`: some slab and group has all 5 slots live in every draw.
All inputs are finite; a program needn't handle non-finite values.
Results may differ from a plain program's by a relative error of at most 0.0025.
Values may be sent and summed in bfloat16 or wider, within the bound.
No kernel may reach another device: no remote copies, remote signals or barrier semaphores. Data moves between devices by JAX's collectives and lax.ppermute only.
A program may use at most 64 MiB of HBM per device.

v0:
```python
import jax
import jax.numpy as jnp
from jax import lax
from jax.sharding import PartitionSpec as P

SENSORS = 1024
SAMPLES = 2048
SB = 16
WIN = 64
K_MAX = 5
TAPS = ((-2, 1.0 / 12.0), (-1, -8.0 / 12.0), (1, 8.0 / 12.0), (2, -1.0 / 12.0))
STEP_SIZE = 0.25
TV_WEIGHT = 0.3
TV_EPS = 0.01


def extended(array, sides, width):
    for axis, dim in sides:
        count, length = (lax.axis_size(axis), array.shape[dim])
        up = [(i, (i + 1) % count) for i in range(count - 1)]
        down = [(j, i) for i, j in up]
        last = lax.slice_in_dim(array, length - width, length, axis=dim)
        initial = lax.slice_in_dim(array, 0, width, axis=dim)
        before = lax.ppermute(last, axis, up)
        after = lax.ppermute(initial, axis, down)
        array = jnp.concatenate([before, array, after], axis=dim)
    return array


def derivative(signal):
    length_t = signal.shape[-1]
    padded = jnp.pad(signal, [(0, 0)] * (signal.ndim - 1) + [(2, 2)])
    summed = jnp.zeros_like(signal)
    for shift_by, coefficient in TAPS:
        summed = summed + coefficient * padded[..., 2 + shift_by : 2 + shift_by + length_t]
    return summed


def forward_step(volume, axis_dim):
    length_a = volume.shape[axis_dim]
    ahead = jnp.concatenate(
        [
            lax.slice_in_dim(volume, 1, length_a, axis=axis_dim),
            lax.slice_in_dim(volume, length_a - 1, length_a, axis=axis_dim),
        ],
        axis=axis_dim,
    )
    return ahead - volume


def backward_shift(field, axis_dim):
    length_a = field.shape[axis_dim]
    zero_row = jnp.zeros_like(lax.slice_in_dim(field, 0, 1, axis=axis_dim))
    return jnp.concatenate(
        [zero_row, lax.slice_in_dim(field, 0, length_a - 1, axis=axis_dim)], axis=axis_dim
    )


def place_window(partial_value, piece, block_index, start):
    corner = (block_index * SB, start)
    current = lax.dynamic_slice(partial_value, corner, (SB, WIN))
    return lax.dynamic_update_slice(partial_value, current + piece, corner)


def slab_tv(image):
    planes_ext = extended(image, (("vox", 0),), 1)
    slab_planes = image.shape[0]
    is_first = lax.axis_index("vox") == 0
    is_last = lax.axis_index("vox") == lax.axis_size("vox") - 1
    plane_index = jnp.arange(slab_planes + 1)[:, None, None]
    lower = planes_ext[:-1]
    step_z = planes_ext[1:] - planes_ext[:-1]
    step_z = jnp.where(is_last & (plane_index == slab_planes), 0.0, step_z)
    step_y = forward_step(lower, 1)
    step_x = forward_step(lower, 2)
    magnitude = jnp.sqrt(step_z * step_z + step_y * step_y + step_x * step_x + TV_EPS)
    unit_z = jnp.where(is_first & (plane_index == 0), 0.0, step_z / magnitude)
    unit_y = step_y / magnitude
    unit_x = step_x / magnitude
    result = unit_z[:-1] - unit_z[1:]
    result = result + (backward_shift(unit_y, 1) - unit_y)[1:]
    result = result + (backward_shift(unit_x, 2) - unit_x)[1:]
    return result


def on_device(image, weights, block_ids, offsets, counts, measured):
    voxels = image.astype(jnp.bfloat16).reshape(-1)
    blocks = weights[0, 0]
    block_index = block_ids[0, 0]
    starts = offsets[0, 0]
    live_count = counts[0, 0]
    group_sens = SENSORS // lax.axis_size("sen")
    live = (jnp.arange(K_MAX) < live_count).astype(jnp.float32)
    pieces = (
        jnp.einsum("v,kvc->kc", voxels, blocks, preferred_element_type=jnp.float32) * live[:, None]
    )

    def cut_window(source, block_number, start):
        corner = (block_number * SB, start)
        return lax.dynamic_slice(source, corner, (SB, WIN)).reshape(SB * WIN)

    zero_partial = jnp.zeros((group_sens, SAMPLES), jnp.float32)

    def add_masked(slot, partial_value):
        return place_window(
            partial_value, pieces[slot].reshape(SB, WIN), block_index[slot], starts[slot]
        )

    partial_value = lax.fori_loop(0, K_MAX, add_masked, zero_partial)
    whole_measured = lax.all_gather(measured, "vox", axis=1, tiled=True)
    summed = lax.psum(partial_value[None], "vox")
    residual_all = derivative(summed) - whole_measured.astype(jnp.float32)
    adjoint_all = (-derivative(residual_all)).astype(jnp.bfloat16)[0]
    own_rows = measured.shape[1]
    residual = lax.dynamic_slice_in_dim(residual_all, lax.axis_index("vox") * own_rows, own_rows, 1)
    windows = jax.vmap(lambda number, start: cut_window(adjoint_all, number, start))(
        block_index, starts
    )
    windows = windows * live.astype(jnp.bfloat16)[:, None]
    grad_local = jnp.einsum("kc,kvc->v", windows, blocks, preferred_element_type=jnp.float32)
    backprojected = lax.psum(grad_local, "sen").reshape(image.shape)
    image_next = image - STEP_SIZE * (backprojected + TV_WEIGHT * slab_tv(image))
    return (image_next, residual)


def solution(mesh):
    placed = (
        P("vox", None, None),
        P("vox", "sen", None, None, None),
        P("vox", "sen", None),
        P("vox", "sen", None),
        P("vox", "sen"),
        P("sen", "vox", None),
    )
    return jax.shard_map(
        on_device,
        mesh=mesh,
        in_specs=placed,
        out_specs=(P("vox", None, None), P("sen", "vox", None)),
        check_vma=False,
    )
```

profile of v0, /device:TPU:1, one launch (start us, length us, event | category | flops | bytes accessed | tf_op | source)
XLA Modules:
  0.0 1128.4 jit_solution(18124372229311792243)
XLA Ops:
  7.2 4.4 collective-permute-start.1
  11.6 1.4 copy.10
  13.7 0.8 constant_dynamic-update-slice_fusion
  14.5 5.5 fusion.2
  20.6 22.0 %while.14 = (s32[]{:T(128)}, f32[256,2048]{1,0:T(8,128)S(1)}, s32[5]{0:T(128)S(1)}, s32[5]{0:T(128)S(1)}, f32[5,1024]{1,0:T(8,128)S(1)}, /*index=5*/s32[]{:T(128)}, s32[1]{0:T(128)}, s32[]{:T(128)}, s32[]{:T(128)}, s32[]{:T(128)}) while((s32[]{:T(128)}, f32[256,2048]{1,0:T(8,128)S(1)}, s32[5]{0:T(128)S(1)}, s32[5]{0:T(128)S(1)}, ...), condition=%wide.region_1.0_spmd, body=%wide.region_0.0_spmd.sunk | while | flops 1033 | bytes 37093 | solution.py:109
  28.4 0.9 dynamic_update_slice.8
  32.8 0.9 dynamic_update_slice.8
  37.3 0.9 dynamic_update_slice.8
  41.7 0.9 dynamic_update_slice.8
  42.7 1.3 copy-done
  44.0 1.3 collective-permute-start
  45.5 3.6 collective-permute-done
  49.3 273.7 %all-gather.2.cloned.1.call-done = bf16[1,256,2048]{2,0,1:T(2,128)(2,1)} async-done(((bf16[1,4,2048]{2,0,1:T(2,128)(2,1)}), bf16[1,256,2048]{2,0,1:T(2,128)(2,1)}) %all-gather.2.cloned.1.call-update) | async-done | bytes 1048592 | tf_op jit(solution)/shard_map/all_gather | solution.py:110
  323.0 717.5 %all-reduce.6.cloned.1.call-done = f32[1,256,2048]{2,1,0:T(8,128)} async-done(((f32[1,256,2048]{2,1,0:T(8,128)}), f32[1,256,2048]{2,1,0:T(8,128)}) %all-reduce.6.cloned.1.call-update) | async-done | bytes 2097168 | tf_op jit(solution)/shard_map/psum | solution.py:111
  1040.5 6.5 convert_subtract_fusion
  1047.0 2.2 fusion.6
  1049.2 10.0 while.15
  1049.9 1.4 bitcast_dynamic-update-slice_fusion.2
  1051.9 1.4 bitcast_dynamic-update-slice_fusion.2
  1053.9 1.4 bitcast_dynamic-update-slice_fusion.2
  1055.8 1.4 bitcast_dynamic-update-slice_fusion.2
  1057.8 1.4 bitcast_dynamic-update-slice_fusion.2
  1059.4 6.8 fusion
  1066.2 54.1 %psum.15 = f32[1,2,512]{2,1,0:T(2,128)S(1)} all-reduce(f32[1,2,512]{2,1,0:T(2,128)S(1)} %reshape.88), channel_id=1, replica_groups=mesh['vox'=64,'sen'=4] {'sen'}, use_global_device_ids=true, to_apply=%region_3.4 | all-reduce | flops 1024 | bytes 8192 | tf_op jit(solution)/shard_map/psum | solution.py:121
  (68 shorter events, 12.9 us)
Async XLA Ops:
  7.2 315.8 %all-gather.2.cloned.1.call-start = ((), (), s32[]{:S(2)}) async-start(), calls=%async_computation.1 | async-start | bytes 2129920 | tf_op jit(solution)/shard_map/all_gather | solution.py:110
  7.2 6.5 collective-permute-start.1
  13.0 1027.5 %all-reduce.6.cloned.1.call-start = ((), (), s32[]{:S(2)}) async-start(), calls=%async_computation | async-start | bytes 4194304 | tf_op jit(solution)/shard_map/psum | solution.py:111
  19.9 0.7 copy-start.2
  19.9 0.7 copy-start.3
  20.0 24.0 %copy-start.1 = (f32[1,2,512]{2,1,0:T(2,128)S(1)}, f32[1,2,512]{2,1,0:T(2,128)}, u32[]{:S(2)}) copy-start(f32[1,2,512]{2,1,0:T(2,128)} %param.8) | copy-start | bytes 12292
  42.7 1.3 copy-start
  44.0 5.1 collective-permute-start
Sparse Core Ops, SparseCore 0:
  13.1 309.8 all-gather.1
  325.6 714.8 all-reduce.5
where the time goes:
time: 1130 us
  waiting for transfers between devices  995 us (88%)
  blocking collectives  54.1 us (5%)
  local copies, waits for them, and re-layouts  24.6 us (2%)
  between operations  14.8 us (1%)
  matrix products  12.3 us (1%)
    psum x1, waiting for transfers between devices, on_device(): summed = lax.psum(partial_value[None], 'vox')  718 us
    all_gather x1, waiting for transfers between devices, on_device(): whole_measured = lax.all_gather(measured, 'vox', axis=1, tiled=True)  274 us
    psum x1, blocking collectives, on_device(): backprojected = lax.psum(grad_local, 'sen').reshape(image.shape)  54.1 us
  transfers between devices with their start and end apart: 4, of which 3 were waited for; matrix products, arithmetic and copies ran while one was open for 2% of the time, Pallas kernels for 0%

commit v1 on v0

--- a/solution.py
+++ b/solution.py
@@ -107,7 +107,15 @@
         )
 
     partial_value = lax.fori_loop(0, K_MAX, add_masked, zero_partial)
-    whole_measured = lax.all_gather(measured, "vox", axis=1, tiled=True)
+    whole_measured = jnp.concatenate(
+        lax.all_to_all(
+            jnp.stack([measured for _ in range(lax.psum(1, axis_name="vox"))]),
+            axis_name="vox",
+            split_axis=0,
+            concat_axis=0,
+        ),
+        axis=1,
+    )
     summed = lax.psum(partial_value[None], "vox")
     residual_all = derivative(summed) - whole_measured.astype(jnp.float32)
     adjoint_all = (-derivative(residual_all)).astype(jnp.bfloat16)[0]

time: 1130 us -> 816 us (0.72)
  waiting for transfers between devices: 995 us -> 666 us
  starting transfers between devices: 5.74 us -> 17.7 us
    all_gather x1 -> x0, waiting for transfers between devices: 274 us -> none  [on_device(): whole_measured = lax.all_gather(measured, 'vox', axis=1, tiled=True)]
    psum x1, waiting for transfers between devices: 718 us -> 635 us  [on_device(): summed = lax.psum(partial_value[None], 'vox')]
    all_to_all x0 -> x1, waiting for transfers between devices: none -> 21.8 us  [on_device(): lax.all_to_all(jnp.stack([measured for _ in range(lax.psum(1, axis_name='...]
    all_to_all x0 -> x1, starting transfers between devices: none -> 11.9 us  [on_device(): lax.all_to_all(jnp.stack([measured for _ in range(lax.psum(1, axis_name='...]
  transfers between devices with their start and end apart: 4 -> 4, of which waited for: 3 -> 4; matrix products, arithmetic and copies ran while one was open for 2% -> 0% of each run, Pallas kernels for 0% -> 0%
where the time goes in v1:
time: 816 us; the launch traced here: 815 us
  waiting for transfers between devices  666 us (82%)
  blocking collectives  54.1 us (7%)
  local copies, waits for them, and re-layouts  26.6 us (3%)
  starting transfers between devices  17.7 us (2%)
  between operations  14.8 us (2%)
  loops' own time  12.9 us (2%)
  matrix products  12.3 us (2%)
  other arithmetic  10.7 us (1%)
    psum x1, waiting for transfers between devices, on_device(): summed = lax.psum(partial_value[None], 'vox')  635 us
    psum x1, blocking collectives, on_device(): backprojected = lax.psum(grad_local, 'sen').reshape(image.shape)  54.1 us
    all_to_all x1, waiting for transfers between devices, on_device(): lax.all_to_all(jnp.stack([measured for _ in range(lax.psum(1, axis_name='...  21.8 us
  transfers between devices with their start and end apart: 4, of which 4 were waited for; matrix products, arithmetic and copies ran while one was open for 0% of the time, Pallas kernels for 0%

profile of v1, /device:TPU:1, one launch (start us, length us, event | category | flops | bytes accessed | tf_op | source)
XLA Modules:
  0.0 815.2 jit_solution(1939579133420188202)
XLA Ops:
  7.2 4.4 collective-permute-start.1
  13.3 5.5 fusion.2
  19.5 24.3 %while.14 = (s32[]{:T(128)}, f32[256,2048]{1,0:T(8,128)S(1)}, s32[5]{0:T(128)S(1)}, s32[5]{0:T(128)S(1)}, f32[5,1024]{1,0:T(8,128)S(1)}, /*index=5*/s32[]{:T(128)}, s32[1]{0:T(128)}, s32[]{:T(128)}, s32[]{:T(128)}, s32[]{:T(128)}) while((s32[]{:T(128)}, f32[256,2048]{1,0:T(8,128)S(1)}, s32[5]{0:T(128)S(1)}, s32[5]{0:T(128)S(1)}, ...), condition=%wide.region_1.0_spmd, body=%wide.region_0.0_spmd.sunk | while | flops 1033 | bytes 37085 | solution.py:109
  28.2 0.9 dynamic_update_slice.8
  33.0 0.9 dynamic_update_slice.8
  37.9 0.9 dynamic_update_slice.8
  43.8 1.3 copy-done
  45.1 1.5 stack.2
  46.6 11.9 %all-to-all-start = ((bf16[64,1,4,2048]{3,2,1,0:T(4,128)(2,1)}), bf16[64,1,4,2048]{3,2,1,0:T(4,128)(2,1)S(1)}, u32[]{:S(2)}, u32[]{:S(2)}) async-start(bf16[64,1,4,2048]{3,2,1,0:T(4,128)(2,1)} %stack.2), calls=%async_computation | async-start | bytes 2097152 | tf_op jit(solution)/shard_map/all_to_all | solution.py:111
  58.6 1.3 collective-permute-start
  60.1 8.7 %collective-permute-done = f32[1,2,512]{2,1,0:T(2,128)S(1)} collective-permute-done((f32[1,2,512]{2,1,0:T(2,128)S(1)}, f32[1,2,512]{2,1,0:T(2,128)S(1)}, u32[]{:S(2)}, u32[]{:S(2)}) %collective-permute-start) | collective-permute-done | bytes 4128 | tf_op jit(solution)/shard_map/ppermute | solution.py:25
  69.0 21.8 %all-to-all-done = bf16[64,1,4,2048]{3,2,1,0:T(4,128)(2,1)S(1)} async-done(((bf16[64,1,4,2048]{3,2,1,0:T(4,128)(2,1)}), bf16[64,1,4,2048]{3,2,1,0:T(4,128)(2,1)S(1)}, u32[]{:S(2)}, u32[]{:S(2)}) %all-to-all-start) | async-done | bytes 1048608 | tf_op jit(solution)/shard_map/all_to_all | solution.py:111
  90.8 1.4 reshape.126
  92.2 635.3 %all-reduce.6.cloned.1.call-done = f32[1,256,2048]{2,1,0:T(8,128)} async-done(((f32[1,256,2048]{2,1,0:T(8,128)}), f32[1,256,2048]{2,1,0:T(8,128)}) %all-reduce.6.cloned.1.call-update) | async-done | bytes 2097168 | tf_op jit(solution)/shard_map/psum | solution.py:119
  727.5 6.3 add_subtract_fusion
  733.7 2.2 fusion.6
  736.0 10.0 %while.15 = (s32[]{:T(128)}, bf16[256,2048]{1,0:T(8,128)(2,1)S(1)}, s32[5,2]{0,1:T(2,128)S(1)}, bf16[5,16,64]{2,1,0:T(8,128)(2,1)S(1)}, s32[]{:T(128)}) while((s32[]{:T(128)}, bf16[256,2048]{1,0:T(8,128)(2,1)S(1)}, s32[5,2]{0,1:T(2,128)S(1)}, bf16[5,16,64]{2,1,0:T(8,128)(2,1)S(1)}, s32[]{:T(128)}) %tuple.55), condition=%wide.while_cond, body=%wide.while_body.sunk | while | flops 2 | bytes 8301 | solution.py:100
  736.6 1.4 bitcast_dynamic-update-slice_fusion.2
  738.6 1.4 bitcast_dynamic-update-slice_fusion.2
  740.6 1.4 bitcast_dynamic-update-slice_fusion.2
  742.6 1.4 bitcast_dynamic-update-slice_fusion.2
  744.6 1.4 bitcast_dynamic-update-slice_fusion.2
  746.1 6.8 fusion
  752.9 54.1 %psum.15 = f32[1,2,512]{2,1,0:T(2,128)S(1)} all-reduce(f32[1,2,512]{2,1,0:T(2,128)S(1)} %reshape.106), channel_id=1, replica_groups=mesh['vox'=64,'sen'=4] {'sen'}, use_global_device_ids=true, to_apply=%region_3.4 | all-reduce | flops 1024 | bytes 8192 | tf_op jit(solution)/shard_map/psum | solution.py:129
  (70 shorter events, 15.3 us)
Async XLA Ops:
  7.2 720.3 %all-reduce.6.cloned.1.call-start = ((), (), s32[]{:S(2)}) async-start(), calls=%async_computation.1 | async-start | bytes 4194304 | tf_op jit(solution)/shard_map/psum | solution.py:119
  7.2 5.3 collective-permute-start.1
  18.8 0.7 copy-start.3
  18.8 0.7 copy-start.4
  18.9 26.3 %copy-start.2 = (bf16[1,4,2048]{2,1,0:T(4,128)(2,1)S(1)}, bf16[1,4,2048]{2,1,0:T(4,128)(2,1)}, u32[]{:S(2)}) copy-start(bf16[1,4,2048]{2,1,0:T(4,128)(2,1)} %param.13) | copy-start | bytes 49156
  43.8 1.3 copy-start
  45.1 13.5 %copy-start.1 = (f32[1,2,512]{2,1,0:T(2,128)S(1)}, f32[1,2,512]{2,1,0:T(2,128)}, u32[]{:S(2)}) copy-start(f32[1,2,512]{2,1,0:T(2,128)} %param.8) | copy-start | bytes 12292
  46.6 44.1 %all-to-all-start = ((bf16[64,1,4,2048]{3,2,1,0:T(4,128)(2,1)}), bf16[64,1,4,2048]{3,2,1,0:T(4,128)(2,1)S(1)}, u32[]{:S(2)}, u32[]{:S(2)}) async-start(bf16[64,1,4,2048]{3,2,1,0:T(4,128)(2,1)} %stack.2), calls=%async_computation | async-start | bytes 2097152 | tf_op jit(solution)/shard_map/all_to_all | solution.py:111
  58.6 10.2 %collective-permute-start = (f32[1,2,512]{2,1,0:T(2,128)S(1)}, f32[1,2,512]{2,1,0:T(2,128)S(1)}, u32[]{:S(2)}, u32[]{:S(2)}) collective-permute-start(f32[1,2,512]{2,1,0:T(2,128)S(1)} %copy-done.1), channel_id=1, source_target_pairs={{4,0},{8,4},{12,8},{16,12},{20,16},{24,20},{28,24},{32,28},{36,32}... | collective-permute-start | bytes 12296 | tf_op jit(solution)/shard_map/ppermute | solution.py:25
Sparse Core Ops, SparseCore 0:
  45.2 682.1 all-reduce.5
